TPU v7x, 128 devices: a whole 4x4x4 slice. The times are simulated.
128 devices in a mesh: grp: 8 (over y, z_hi), ctx: 16 (over x, z_lo, core).
Axes of the slice: x: 4, y: 4, z: 4 (z_hi: 2, z_lo: 2; z = z_hi * 2 + z_lo), core: 2. Of those that a mesh axis runs over, the one named last changes fastest.
Arguments:
- tokens: bfloat16 [16384, 2048], P(('grp', 'ctx')), may hold values from -3 to 3
- queries: bfloat16 [16384, 4096], P(('grp', 'ctx')), may hold values from -6 to 6
- keys_values: bfloat16 [8, 4096, 1024], P('grp', 'ctx'), may hold values from -600 to 600
- out_weight: bfloat16 [4096, 2048], P('grp'), may hold values from -1 to 1
- moe_gain: float32 [2048], replicated, may hold values from 0.1 to 1.9
- expert_ids: int32 [16384, 8], P(('grp', 'ctx')), may hold values from 0 to 127, all different within a row; in each aligned block of 128 rows (0 to 127, 128 to 255, ...) at most 12 rows name the same one
- gates: float32 [16384, 8], P(('grp', 'ctx')), may hold values from 0.05 to 0.3
- w_gate_experts: bfloat16 [128, 2048, 768], P(('grp', 'ctx')), may hold values from -0.125 to 0.125
- w_up_experts: bfloat16 [128, 2048, 768], P(('grp', 'ctx')), may hold values from -0.125 to 0.125
- w_down_experts: bfloat16 [128, 768, 2048], P(('grp', 'ctx')), may hold values from -0.21875 to 0.21875
Outputs:
- layer_out: bfloat16 [16384, 2048], P(('grp', 'ctx'))
Inputs may be any that keep to these rules, and one draw needn't show every extreme that they name: `expert_ids`: each row names 8 different experts; among the 128 rows of one device no expert is named more than 12 times, a bound that some block reaches.
All inputs are finite; a program needn't handle non-finite values.
Results may differ from a plain program's by a relative error of at most 0.015.
Values may be sent and summed in bfloat16 or wider, within the bound.
A program may use at most 128 MiB of HBM per device.

v0:
```python
import math

import jax
import jax.numpy as jnp
from jax import lax
from jax.sharding import PartitionSpec as P

H = 32
KV_HEADS = 4
HEAD_DIM = 128
EXPERTS = 128
TOPK = 8
CAP = 12


masked_score = -1e30


def softmax_step(running, grouped, key_block, value_block, key_position, query_position, scaling):
    top_score, total_weight, weighted = running
    scores = (
        jnp.einsum("gqd,gkd->gqk", grouped, key_block, preferred_element_type=jnp.float32) * scaling
    )
    allowed = key_position[None, None, :] <= query_position[None, :, None]
    scores = jnp.where(allowed, scores, masked_score)
    fresh_top = jnp.maximum(top_score, jnp.max(scores, axis=2))
    weights = jnp.where(allowed, jnp.exp(scores - fresh_top[:, :, None]), 0.0).astype(jnp.bfloat16)
    factor = jnp.exp(top_score - fresh_top)
    total_weight = total_weight * factor + jnp.sum(weights, axis=2, dtype=jnp.float32)
    weighted = weighted * factor[:, :, None] + jnp.einsum(
        "gqk,gkd->gqd", weights, value_block, preferred_element_type=jnp.float32
    )
    return (fresh_top, total_weight, weighted)


def per_device(
    tokens,
    queries,
    keys_values,
    out_weight,
    moe_gain,
    expert_ids,
    gates,
    w_gate_experts,
    w_up_experts,
    w_down_experts,
):
    tok_count = tokens.shape[0]
    ctx_count = lax.axis_size("ctx")
    kv_width = keys_values.shape[2] // 2
    group_heads = H // KV_HEADS
    keys_total = keys_values.shape[1] * ctx_count
    query_position = (
        keys_total
        - tok_count * ctx_count
        + lax.axis_index("ctx") * tok_count
        + jnp.arange(tok_count, dtype=jnp.int32)
    )
    query_tiled = jnp.tile(query_position, group_heads)
    grouped = (
        queries.reshape(tok_count, KV_HEADS, group_heads, HEAD_DIM)
        .transpose(1, 2, 0, 3)
        .reshape(KV_HEADS, group_heads * tok_count, HEAD_DIM)
    )
    scaling = 1.0 / math.sqrt(HEAD_DIM)
    query_rows = group_heads * tok_count
    initial = (
        jnp.full((KV_HEADS, query_rows), masked_score, jnp.float32),
        jnp.zeros((KV_HEADS, query_rows), jnp.float32),
        jnp.zeros((KV_HEADS, query_rows, HEAD_DIM), jnp.float32),
    )
    piece = lax.all_gather(keys_values, "ctx", axis=1, tiled=True)
    length = piece.shape[1]
    block_size = 1024

    def one_block(index, state):
        offset = index * block_size
        window = lax.dynamic_slice_in_dim(piece[0], offset, block_size, 0)
        key_block = window[:, :kv_width].reshape(block_size, KV_HEADS, HEAD_DIM).transpose(1, 0, 2)
        value_block = (
            window[:, kv_width:].reshape(block_size, KV_HEADS, HEAD_DIM).transpose(1, 0, 2)
        )
        key_position = offset + jnp.arange(block_size, dtype=jnp.int32)
        return softmax_step(
            state, grouped, key_block, value_block, key_position, query_tiled, scaling
        )

    top_score, total_weight, weighted = lax.fori_loop(0, length // block_size, one_block, initial)
    attended = (
        (weighted / total_weight[:, :, None])
        .reshape(KV_HEADS, group_heads, tok_count, HEAD_DIM)
        .transpose(2, 0, 1, 3)
        .reshape(tok_count, H * HEAD_DIM)
        .astype(jnp.bfloat16)
    )
    head_parts = lax.all_to_all(attended, "grp", split_axis=1, concat_axis=0, tiled=True)
    projected = lax.psum_scatter(
        jnp.dot(head_parts, out_weight, preferred_element_type=jnp.float32).astype(jnp.bfloat16),
        "grp",
        scatter_dimension=0,
        tiled=True,
    ).astype(jnp.float32)
    residual = (tokens.astype(jnp.float32) + projected).astype(jnp.bfloat16)
    wide = residual.astype(jnp.float32)
    normed = (
        wide * lax.rsqrt(jnp.mean(wide * wide, axis=1, keepdims=True) + 1e-06) * moe_gain
    ).astype(jnp.bfloat16)
    flat_ids = expert_ids.reshape(-1)
    one_hot = (flat_ids[:, None] == jnp.arange(EXPERTS, dtype=jnp.int32)[None, :]).astype(jnp.int32)
    slot_index = jnp.sum((jnp.cumsum(one_hot, axis=0) - one_hot) * one_hot, axis=1)
    position = flat_ids * CAP + slot_index
    token_index = jnp.arange(tok_count * TOPK, dtype=jnp.int32) // TOPK
    table = jnp.full((EXPERTS * CAP,), tok_count, jnp.int32).at[position].set(token_index)
    present = table < tok_count
    outgoing = jnp.where(present[:, None], normed[jnp.minimum(table, tok_count - 1)], 0.0)
    local_experts = w_gate_experts.shape[0]
    owners = EXPERTS // local_experts
    width = normed.shape[1]
    outgoing = outgoing.reshape(owners, local_experts, CAP, width)
    incoming = lax.all_to_all(outgoing, ("grp", "ctx"), split_axis=0, concat_axis=0, tiled=True)
    gate_part = jnp.einsum(
        "sjcd,jdf->sjcf", incoming, w_gate_experts, preferred_element_type=jnp.float32
    )
    up_part = jnp.einsum(
        "sjcd,jdf->sjcf", incoming, w_up_experts, preferred_element_type=jnp.float32
    )
    hidden = (jax.nn.silu(gate_part) * up_part).astype(jnp.bfloat16)
    result_rows = jnp.einsum(
        "sjcf,jfd->sjcd", hidden, w_down_experts, preferred_element_type=jnp.float32
    ).astype(jnp.bfloat16)
    returned = lax.all_to_all(result_rows, ("grp", "ctx"), split_axis=0, concat_axis=0, tiled=True)
    picked = returned.reshape(EXPERTS * CAP, width)[position].reshape(tok_count, TOPK, width)
    combined = jnp.sum(picked.astype(jnp.float32) * gates[:, :, None], axis=1)
    return (wide + combined).astype(jnp.bfloat16)


def solution(mesh):
    return jax.shard_map(
        per_device,
        mesh=mesh,
        in_specs=(
            P(("grp", "ctx"), None),
            P(("grp", "ctx"), None),
            P("grp", "ctx", None),
            P("grp", None),
            P(),
            P(("grp", "ctx"), None),
            P(("grp", "ctx"), None),
            P(("grp", "ctx"), None, None),
            P(("grp", "ctx"), None, None),
            P(("grp", "ctx"), None, None),
        ),
        out_specs=P(("grp", "ctx"), None),
        check_vma=False,
    )
```

profile of v0, /device:TPU:4, one launch (start us, length us, event | category | flops | bytes accessed | tf_op | source)
XLA Modules:
  0.0 684.7 jit_solution(3027058764140769704)
XLA Ops:
  11.7 60.1 %all-gather.2.cloned.1.call-done = bf16[1,4096,1024]{1,2,0:T(8,128)(2,1)} async-done(((bf16[1,256,1024]{1,2,0:T(8,128)(2,1)}), bf16[1,4096,1024]{1,2,0:T(8,128)(2,1)}) %all-gather.2.cloned.1.call-update) | async-done | bytes 8388624 | tf_op jit(solution)/shard_map/all_gather | solution.py:72
  71.8 153.5 %while.18 = (s32[]{:T(128)}, f32[4,1024]{1,0:T(4,128)S(1)}, f32[4,1024]{1,0:T(4,128)S(1)}, f32[4,1024,128]{2,1,0:T(8,128)}, bf16[1,4096,1024]{1,2,0:T(8,128)(2,1...) while((s32[]{:T(128)}, f32[4,1024]{1,0:T(4,128)S(1)}, ...), condition=%wide.region_3.4_spmd.clone, body=%wide.region_0.3_spmd.clone.sunk | while | flops 2213041152 | bytes 78922440 | solution.py:88
  78.1 10.7 %fusion.52 = (f32[4,1024]{1,0:T(4,128)S(1)}, f32[4,1024,1024]{2,1,0:T(8,128)}) fusion(pred[1024,1024]{0,1:T(8,128)(4,1)S(1)} %broadcast_compare_fusion.3, bf16[4,1024,128]{2,1,0:T(8,128)(2,1)} %get-tuple-element.261, bf16[1024,4,128]{2,0,1:T(8,128)(2,1)} %copy.73), kind=kOutput, calls=%fused_computation.7.clone.1 | convolution fusion | flops 1086320640 | bytes 19939328 | tf_op jit(solution)/shard_map/while/body/eval_jaxpr/gqd,gkd->gqk/dot_general | solution.py:22
  88.8 8.1 %convert_reduce_fusion.2 = f32[4,1024]{1,0:T(4,128)S(1)} fusion(f32[4,1024]{1,0:T(4,128)S(1)} %select_maximum_fusion.2, f32[4,1024,1024]{2,1,0:T(8,128)} %get-tuple-element.230, pred[1024,1024]{0,1:T(8,128)(4,1)} %copy-done.1), kind=kLoop, calls=%fused_computation.5.clone.1 | loop fusion | flops 29356032 | bytes 17858560 | tf_op jit(solution)/shard_map/while/body/eval_jaxpr/reduce_sum | solution.py:29
  99.2 10.7 %fusion.54 = f32[4,1024,128]{2,1,0:T(8,128)} fusion(f32[4,1024,128]{2,1,0:T(8,128)} %get-tuple-element.248, bf16[1024,4,128]{2,0,1:T(8,128)(2,1)} %copy.74, f32[4,1024]{1,0:T(4,128)S(1)} %get-tuple-element.233, pred[]{:T(512)S(6)} %compare.5, f32[4,1024,1024]{2,1,0:T(8,128)} %get-tuple-element.230, f32[4,1024]{1,0:T(4,128)S(1)} %select_maximum_fusion.2, ...), kind=kOutput, calls=%fused_computation.9.clone.1 | convolution fusion | flops 1096286208 | bytes 23101440 | tf_op jit(solution)/shard_map/while/body/eval_jaxpr/gqk,gkd->gqd/dot_general | solution.py:30
  116.2 10.7 %fusion.52 = (f32[4,1024]{1,0:T(4,128)S(1)}, f32[4,1024,1024]{2,1,0:T(8,128)}) fusion(pred[1024,1024]{0,1:T(8,128)(4,1)S(1)} %broadcast_compare_fusion.3, bf16[4,1024,128]{2,1,0:T(8,128)(2,1)} %get-tuple-element.261, bf16[1024,4,128]{2,0,1:T(8,128)(2,1)} %copy.73), kind=kOutput, calls=%fused_computation.7.clone.1 | convolution fusion | flops 1086320640 | bytes 19939328 | tf_op jit(solution)/shard_map/while/body/eval_jaxpr/gqd,gkd->gqk/dot_general | solution.py:22
  126.9 8.1 %convert_reduce_fusion.2 = f32[4,1024]{1,0:T(4,128)S(1)} fusion(f32[4,1024]{1,0:T(4,128)S(1)} %select_maximum_fusion.2, f32[4,1024,1024]{2,1,0:T(8,128)} %get-tuple-element.230, pred[1024,1024]{0,1:T(8,128)(4,1)} %copy-done.1), kind=kLoop, calls=%fused_computation.5.clone.1 | loop fusion | flops 29356032 | bytes 17858560 | tf_op jit(solution)/shard_map/while/body/eval_jaxpr/reduce_sum | solution.py:29
  137.3 11.0 %fusion.54 = f32[4,1024,128]{2,1,0:T(8,128)} fusion(f32[4,1024,128]{2,1,0:T(8,128)} %get-tuple-element.248, bf16[1024,4,128]{2,0,1:T(8,128)(2,1)} %copy.74, f32[4,1024]{1,0:T(4,128)S(1)} %get-tuple-element.233, pred[]{:T(512)S(6)} %compare.5, f32[4,1024,1024]{2,1,0:T(8,128)} %get-tuple-element.230, f32[4,1024]{1,0:T(4,128)S(1)} %select_maximum_fusion.2, ...), kind=kOutput, calls=%fused_computation.9.clone.1 | convolution fusion | flops 1096286208 | bytes 23101440 | tf_op jit(solution)/shard_map/while/body/eval_jaxpr/gqk,gkd->gqd/dot_general | solution.py:30
  154.7 10.7 %fusion.52 = (f32[4,1024]{1,0:T(4,128)S(1)}, f32[4,1024,1024]{2,1,0:T(8,128)}) fusion(pred[1024,1024]{0,1:T(8,128)(4,1)S(1)} %broadcast_compare_fusion.3, bf16[4,1024,128]{2,1,0:T(8,128)(2,1)} %get-tuple-element.261, bf16[1024,4,128]{2,0,1:T(8,128)(2,1)} %copy.73), kind=kOutput, calls=%fused_computation.7.clone.1 | convolution fusion | flops 1086320640 | bytes 19939328 | tf_op jit(solution)/shard_map/while/body/eval_jaxpr/gqd,gkd->gqk/dot_general | solution.py:22
  165.4 8.1 %convert_reduce_fusion.2 = f32[4,1024]{1,0:T(4,128)S(1)} fusion(f32[4,1024]{1,0:T(4,128)S(1)} %select_maximum_fusion.2, f32[4,1024,1024]{2,1,0:T(8,128)} %get-tuple-element.230, pred[1024,1024]{0,1:T(8,128)(4,1)} %copy-done.1), kind=kLoop, calls=%fused_computation.5.clone.1 | loop fusion | flops 29356032 | bytes 17858560 | tf_op jit(solution)/shard_map/while/body/eval_jaxpr/reduce_sum | solution.py:29
  175.8 11.0 %fusion.54 = f32[4,1024,128]{2,1,0:T(8,128)} fusion(f32[4,1024,128]{2,1,0:T(8,128)} %get-tuple-element.248, bf16[1024,4,128]{2,0,1:T(8,128)(2,1)} %copy.74, f32[4,1024]{1,0:T(4,128)S(1)} %get-tuple-element.233, pred[]{:T(512)S(6)} %compare.5, f32[4,1024,1024]{2,1,0:T(8,128)} %get-tuple-element.230, f32[4,1024]{1,0:T(4,128)S(1)} %select_maximum_fusion.2, ...), kind=kOutput, calls=%fused_computation.9.clone.1 | convolution fusion | flops 1096286208 | bytes 23101440 | tf_op jit(solution)/shard_map/while/body/eval_jaxpr/gqk,gkd->gqd/dot_general | solution.py:30
  193.1 10.7 %fusion.52 = (f32[4,1024]{1,0:T(4,128)S(1)}, f32[4,1024,1024]{2,1,0:T(8,128)}) fusion(pred[1024,1024]{0,1:T(8,128)(4,1)S(1)} %broadcast_compare_fusion.3, bf16[4,1024,128]{2,1,0:T(8,128)(2,1)} %get-tuple-element.261, bf16[1024,4,128]{2,0,1:T(8,128)(2,1)} %copy.73), kind=kOutput, calls=%fused_computation.7.clone.1 | convolution fusion | flops 1086320640 | bytes 19939328 | tf_op jit(solution)/shard_map/while/body/eval_jaxpr/gqd,gkd->gqk/dot_general | solution.py:22
  203.8 8.1 %convert_reduce_fusion.2 = f32[4,1024]{1,0:T(4,128)S(1)} fusion(f32[4,1024]{1,0:T(4,128)S(1)} %select_maximum_fusion.2, f32[4,1024,1024]{2,1,0:T(8,128)} %get-tuple-element.230, pred[1024,1024]{0,1:T(8,128)(4,1)} %copy-done.1), kind=kLoop, calls=%fused_computation.5.clone.1 | loop fusion | flops 29356032 | bytes 17858560 | tf_op jit(solution)/shard_map/while/body/eval_jaxpr/reduce_sum | solution.py:29
  214.2 11.0 %fusion.54 = f32[4,1024,128]{2,1,0:T(8,128)} fusion(f32[4,1024,128]{2,1,0:T(8,128)} %get-tuple-element.248, bf16[1024,4,128]{2,0,1:T(8,128)(2,1)} %copy.74, f32[4,1024]{1,0:T(4,128)S(1)} %get-tuple-element.233, pred[]{:T(512)S(6)} %compare.5, f32[4,1024,1024]{2,1,0:T(8,128)} %get-tuple-element.230, f32[4,1024]{1,0:T(4,128)S(1)} %select_maximum_fusion.2, ...), kind=kOutput, calls=%fused_computation.9.clone.1 | convolution fusion | flops 1096286208 | bytes 23101440 | tf_op jit(solution)/shard_map/while/body/eval_jaxpr/gqk,gkd->gqd/dot_general | solution.py:30
  230.3 23.9 %all_to_all.26 = bf16[128,8,512]{0,2,1:T(8,128)(2,1)} all-to-all(bf16[128,8,512]{0,2,1:T(8,128)(2,1)} %bitcast.136), channel_id=1, replica_groups=mesh['grp'=8,'ctx'=16] {'grp'}, dimensions={1} | all-to-all | bytes 2097152 | tf_op jit(solution)/shard_map/all_to_all | solution.py:96
  272.2 73.5 %reduce-scatter.2.cloned.1.call-done = bf16[128,2048]{1,0:T(8,128)(2,1)} async-done(((bf16[1024,2048]{1,0:T(8,128)(2,1)}), bf16[128,2048]{1,0:T(8,128)(2,1)}) %reduce-scatter.2.cloned.1.call-update) | async-done | bytes 524304 | tf_op jit(solution)/shard_map/reduce_scatter | solution.py:97
  349.4 13.8 %gather_fusion = bf16[1536,2048]{1,0:T(8,128)(2,1)} fusion(bf16[128,2048]{1,0:T(8,128)(2,1)} %fusion.26, s32[2048]{0:T(1024)S(1)} %pad_clamp_fusion), kind=kCustom, calls=%fused_computation | custom fusion | bytes 12589056 | tf_op jit(solution)/shard_map/gather | solution.py:115
  363.2 10.6 %gather.9 = bf16[128,1,12,2048]{3,2,0,1:T(8,128)(2,1)} reshape(bf16[1536,2048]{1,0:T(8,128)(2,1)} %gather_fusion) | data formatting | bytes 12582912 | tf_op jit(solution)/shard_map/gather | solution.py:115
  381.0 109.1 %all_to_all.27 = bf16[128,1,12,2048]{3,2,1,0:T(8,128)(2,1)S(1)} all-to-all(bf16[128,1,12,2048]{3,2,1,0:T(8,128)(2,1)} %select_bitcast_fusion), channel_id=1, replica_groups=mesh['grp'=8,'ctx'=16] {'grp','ctx'}, dimensions={0} | all-to-all | bytes 12582912 | tf_op jit(solution)/shard_map/all_to_all | solution.py:120
  490.2 12.7 %fusion.11 = f32[128,12,768]{2,0,1:T(8,128)S(1)} fusion(bf16[128,1,12,2048]{3,2,1,0:T(8,128)(2,1)S(1)} %all_to_all.27, bf16[1,2048,768]{2,1,0:T(8,128)(2,1)S(1)} %copy-done.8), kind=kOutput, calls=%fused_computation.26 | convolution fusion | flops 4831838208 | bytes 14155776 | tf_op jit(solution)/shard_map/sjcd,jdf->sjcf/dot_general | solution.py:121
  502.9 12.5 %fusion.9 = f32[128,12,768]{2,0,1:T(8,128)S(1)} fusion(bf16[128,1,12,2048]{3,2,1,0:T(8,128)(2,1)S(1)} %all_to_all.27, bf16[1,2048,768]{2,1,0:T(8,128)(2,1)S(1)} %copy-done.9), kind=kOutput, calls=%fused_computation.24 | convolution fusion | flops 4831838208 | bytes 14155776 | tf_op jit(solution)/shard_map/sjcd,jdf->sjcf/dot_general | solution.py:124
  535.0 111.9 %all-to-all-done.2 = bf16[128,1,12,2048]{3,2,1,0:T(8,128)(2,1)} async-done(((bf16[128,1,12,2048]{3,2,1,0:T(8,128)(2,1)}), bf16[128,1,12,2048]{3,2,1,0:T(8,128)(2,1)}, u32[]{:S(2)}, u32[]{:S(2)}) %all-to-all-start.2) | async-done | bytes 6291488 | tf_op jit(solution)/shard_map/all_to_all | solution.py:131
  647.0 10.7 %reshape.189 = bf16[1536,2048]{1,0:T(8,128)(2,1)} reshape(bf16[128,1,12,2048]{3,2,1,0:T(8,128)(2,1)} %all-to-all-done.2) | data formatting | bytes 12582912 | tf_op jit(solution)/shard_map/reshape | solution.py:132
  657.7 12.4 %gather_fusion.1 = bf16[1024,2048]{1,0:T(8,128)(2,1)} fusion(bf16[1536,2048]{1,0:T(8,128)(2,1)} %reshape.189, s32[1024]{0:T(1024)S(1)} %broadcast_clamp_fusion), kind=kCustom, calls=%fused_computation.1 | custom fusion | bytes 8392704 | tf_op jit(solution)/shard_map/gather | solution.py:132
  (113 shorter events, 100.2 us)
Async XLA Ops:
  6.5 509.2 %copy-start = (bf16[1,768,2048]{2,1,0:T(8,128)(2,1)S(1)}, bf16[1,768,2048]{2,1,0:T(8,128)(2,1)}, u32[]{:S(2)}) copy-start(bf16[1,768,2048]{2,1,0:T(8,128)(2,1)} %param.21) | copy-start | bytes 9437188
  6.5 65.3 %all-gather.2.cloned.1.call-start = ((), (), s32[]{:S(2)}) async-start(), calls=%async_computation.4 | async-start | bytes 8912896 | tf_op jit(solution)/shard_map/all_gather | solution.py:72
  8.8 337.0 %reduce-scatter.2.cloned.1.call-start = ((), (), s32[]{:S(2)}) async-start(), calls=%async_computation.5 | async-start | bytes 4718592 | tf_op jit(solution)/shard_map/reduce_scatter | solution.py:97
  78.1 10.7 %copy-start.1 = (pred[1024,1024]{0,1:T(8,128)(4,1)}, pred[1024,1024]{0,1:T(8,128)(4,1)S(1)}, u32[]{:S(2)}) copy-start(pred[1024,1024]{0,1:T(8,128)(4,1)S(1)} %broadcast_compare_fusion.3) | copy-start | bytes 3145732 | tf_op jit(solution)/shard_map/while
  116.2 10.7 %copy-start.1 = (pred[1024,1024]{0,1:T(8,128)(4,1)}, pred[1024,1024]{0,1:T(8,128)(4,1)S(1)}, u32[]{:S(2)}) copy-start(pred[1024,1024]{0,1:T(8,128)(4,1)S(1)} %broadcast_compare_fusion.3) | copy-start | bytes 3145732 | tf_op jit(solution)/shard_map/while
  154.7 10.7 %copy-start.1 = (pred[1024,1024]{0,1:T(8,128)(4,1)}, pred[1024,1024]{0,1:T(8,128)(4,1)S(1)}, u32[]{:S(2)}) copy-start(pred[1024,1024]{0,1:T(8,128)(4,1)S(1)} %broadcast_compare_fusion.3) | copy-start | bytes 3145732 | tf_op jit(solution)/shard_map/while
  193.1 10.7 %copy-start.1 = (pred[1024,1024]{0,1:T(8,128)(4,1)}, pred[1024,1024]{0,1:T(8,128)(4,1)S(1)}, u32[]{:S(2)}) copy-start(pred[1024,1024]{0,1:T(8,128)(4,1)S(1)} %broadcast_compare_fusion.3) | copy-start | bytes 3145732 | tf_op jit(solution)/shard_map/while
  256.4 6.2 copy-start.5
  262.6 84.5 %copy-start.6 = (f32[2048]{0:T(1024)S(1)}, f32[2048]{0:T(1024)}, u32[]{:S(2)}) copy-start(f32[2048]{0:T(1024)} %param.16) | copy-start | bytes 24580
  263.3 0.8 copy-start.4
  381.0 109.1 %copy-start.8 = (bf16[1,2048,768]{2,1,0:T(8,128)(2,1)S(1)}, bf16[1,2048,768]{2,1,0:T(8,128)(2,1)}, u32[]{:S(2)}) copy-start(bf16[1,2048,768]{2,1,0:T(8,128)(2,1)} %param.19) | copy-start | bytes 9437188
  490.2 12.7 %copy-start.9 = (bf16[1,2048,768]{2,1,0:T(8,128)(2,1)S(1)}, bf16[1,2048,768]{2,1,0:T(8,128)(2,1)}, u32[]{:S(2)}) copy-start(bf16[1,2048,768]{2,1,0:T(8,128)(2,1)} %param.20) | copy-start | bytes 9437188
  527.9 7.0 %copy-start.7 = (f32[128,8]{0,1:T(8,128)S(1)}, f32[128,8]{0,1:T(8,128)}, u32[]{:S(2)}) copy-start(f32[128,8]{0,1:T(8,128)} %param.18) | copy-start | bytes 12292
  527.9 119.0 %all-to-all-start.2 = ((bf16[128,1,12,2048]{3,2,1,0:T(8,128)(2,1)}), bf16[128,1,12,2048]{3,2,1,0:T(8,128)(2,1)}, u32[]{:S(2)}, u32[]{:S(2)}) async-start(bf16[128,1,12,2048]{3,2,1,0:T(8,128)(2,1)} %copy.59), calls=%async_computation.3 | async-start | bytes 16777216 | tf_op jit(solution)/shard_map/all_to_all | solution.py:131
  670.1 6.6 copy-start.2
  670.1 6.6 copy-start.3
Sparse Core Ops, SparseCore 0:
  9.0 62.7 all-gather.1
  262.8 82.8 reduce-scatter.1
where the time goes:
time: 694 us; the launch traced here: 685 us
  waiting for transfers between devices  246 us (35%)
  blocking collectives  133 us (19%)
  matrix products  123 us (18%)
  local copies, waits for them, and re-layouts  102 us (15%)
  other arithmetic  59.1 us (9%)
  between operations  14.2 us (2%)
  starting transfers between devices  7.02 us (1%)
    all_to_all x1, waiting for transfers between devices, per_device(): lax.all_to_all(result_rows, ('grp', 'ctx'), split_axis=0, concat_axis=0,...  112 us
    all_to_all x1, blocking collectives, per_device(): lax.all_to_all(outgoing, ('grp', 'ctx'), split_axis=0, concat_axis=0, til...  109 us
    reduce_scatter x1, waiting for transfers between devices, per_device(): lax.psum_scatter(jnp.dot(head_parts, out_weight, preferred_element_type=j...  73.5 us
    all_gather x1, waiting for transfers between devices, per_device(): piece = lax.all_gather(keys_values, 'ctx', axis=1, tiled=True)  60.1 us
    dot_general x4, matrix products, softmax_step(): jnp.einsum('gqk,gkd->gqd', weights, value_block, preferred_element_type=j...  43.9 us
    dot_general x4, matrix products, softmax_step(): jnp.einsum('gqd,gkd->gqk', grouped, key_block, preferred_element_type=jnp...  42.7 us
    reduce_sum x4, other arithmetic, softmax_step(): jnp.sum(weights, axis=2, dtype=jnp.float32)  32.4 us
    gather x2, local copies, waits for them, and re-layouts, per_device(): normed[jnp.minimum(table, tok_count - 1)]  24.4 us
  transfers between devices with their start and end apart: 3, of which 3 were waited for; matrix products, arithmetic and copies ran while one was open for 2% of the time, Pallas kernels for 0%

commit v1 on v0

v1 whole, which is shorter than its diff:
```python
import functools
import math

import jax
import jax.numpy as jnp
from jax import lax
from jax.experimental import pallas as pl
from jax.experimental.pallas import tpu as pltpu
from jax.sharding import PartitionSpec as P

H = 32
KV_HEADS = 4
HEAD_DIM = 128
EXPERTS = 128
TOPK = 8
CAP = 12
D = 2048
TOK = 128
PAIR = 2 * CAP
CHIPS = 64
SLOTS = CHIPS * PAIR
MESH = pl.DeviceIdType.MESH
BF16 = jnp.bfloat16
F32 = jnp.float32


def place():
    g = lax.axis_index("grp")
    c = lax.axis_index("ctx")
    return g, c


def attn_kernel(
    tok_hbm, q_hbm, kv_hbm, w_hbm, gain_ref, ids_ref, gat_ref,
    resid_ref, normed_ref, p_ref, chi_ref, clo_ref,
    kvbuf, qbuf, tokbuf, idsbuf, gatbuf, wbuf, acc, mx, attn, part, sendb, recvb, tmp, valb, gb,
    kv_ssem, kv_rsem, w_ssem, w_rsem, ex_ssem, ex_rsem, pr_ssem, pr_rsem,
):
    g, c = place()
    y, hi = g // 2, g % 2
    x, z, k = c // 4, (c // 2) % 2, c % 2
    j = c // 2

    def dev(xx, zz, kk):
        return (g, ((xx % 4) * 2 + zz) * 2 + kk)

    def wdev(yy, hh, zz):
        return ((yy % 4) * 2 + hh, (x * 2 + zz) * 2 + k)

    def remote(src, dst, ss, rs, device):
        return pltpu.make_async_remote_copy(
            src_ref=src, dst_ref=dst, send_sem=ss, recv_sem=rs, device_id=device, device_id_type=MESH
        )

    partner = dev(x, z, 1 - k)
    up, down = (x + 1) % 4, (x + 3) % 4
    near = [partner]
    for h in range(2):
        near += [dev(up, z, h), dev(down, z, h), dev(x, 1 - z, h)]
    near += [wdev(y + 1, hi, z), wdev(y + 3, hi, z), wdev(y, 1 - hi, 1 - z)]
    barrier = pltpu.get_barrier_semaphore()
    for target in near:
        pl.semaphore_signal(barrier, inc=1, device_id=target, device_id_type=MESH)
    pl.semaphore_wait(barrier, len(near))

    def kv_part(h, kv):
        return kv_hbm.at[0, :, pl.ds(pl.multiple_of(kv * 512 + h * 256, 256), 256)]

    def q_part(h):
        return q_hbm.at[:, pl.ds(pl.multiple_of(h * 2048, 2048), 2048)]

    sends = []

    def push(copy):
        copy.start()
        sends.append(copy)

    locals_ = []

    def pull(copy):
        copy.start()
        locals_.append(copy)

    push(remote(q_part(1 - k), qbuf.at[k], ex_ssem.at[0], ex_rsem.at[0], partner))
    pull(pltpu.make_async_copy(q_part(k), qbuf.at[k], ex_ssem.at[4]))
    for kv in range(2):
        push(remote(kv_part(1 - k, kv), kvbuf.at[j, k, kv], kv_ssem.at[kv], kv_rsem.at[j], partner))
        pltpu.make_async_copy(kv_part(k, kv), kvbuf.at[j, k, kv], kv_rsem.at[j]).start()
    n = 2
    for target in ((up, z), (down, z), (x, 1 - z)):
        for h in range(2):
            for kv in range(2):
                push(remote(kv_part(h, kv), kvbuf.at[j, k, kv], kv_ssem.at[n], kv_rsem.at[j], dev(*target, h)))
                n += 1

    mine = y // 2 == k
    slot_own = (y % 2) * 2 + hi
    slot_own_z = (y % 2) * 2 + 1 - hi
    slot_dn = ((y + 3) % 2) * 2 + hi
    slot_up_z = ((y + 1) % 2) * 2 + 1 - hi
    down_in = ((y + 3) % 4) // 2 == k
    up_in = ((y + 1) % 4) // 2 == k

    def w_copy(src, slot, index, target):
        return remote(src, wbuf.at[slot], w_ssem.at[index], w_rsem.at[slot], target)

    own_sends = [
        w_copy(w_hbm, slot_own, 0, wdev(y, 1 - hi, 1 - z)),
        w_copy(w_hbm, slot_own, 1, wdev(y + 1, hi, z)),
        w_copy(w_hbm, slot_own, 2, wdev(y + 3, hi, z)),
    ]
    z_sends = [
        w_copy(wbuf.at[slot_own_z], slot_own_z, 3, wdev(y + 1, hi, z)),
        w_copy(wbuf.at[slot_own_z], slot_own_z, 4, wdev(y + 3, hi, z)),
    ]
    dn_send = w_copy(wbuf.at[slot_dn], slot_dn, 5, wdev(y + 1, hi, z))
    up_send = w_copy(wbuf.at[slot_up_z], slot_up_z, 6, wdev(y + 3, hi, z))

    def w_arrived(slot):
        return w_copy(wbuf.at[slot], slot, 0, partner)

    @pl.when(mine)
    def _():
        for copy in own_sends:
            copy.start()
        pltpu.make_async_copy(w_hbm, wbuf.at[slot_own], w_rsem.at[slot_own]).start()

    push(remote(tok_hbm, tokbuf.at[k], ex_ssem.at[1], ex_rsem.at[1], partner))
    pull(pltpu.make_async_copy(tok_hbm, tokbuf.at[k], ex_ssem.at[5]))
    push(remote(ids_ref, idsbuf.at[k], ex_ssem.at[2], ex_rsem.at[2], partner))
    pull(pltpu.make_async_copy(ids_ref, idsbuf.at[k], ex_ssem.at[6]))
    push(remote(gat_ref, gatbuf.at[k], ex_ssem.at[3], ex_rsem.at[3], partner))
    pull(pltpu.make_async_copy(gat_ref, gatbuf.at[k], ex_ssem.at[7]))

    acc[...] = jnp.zeros_like(acc)
    mx[...] = jnp.full_like(mx, -1e30)

    sends[0].wait_recv()
    locals_[0].wait()

    factor = math.log2(math.e) / math.sqrt(HEAD_DIM)

    def head(h, js, masked):
        cols = pl.ds(pl.multiple_of(h * 128, 128), 128)
        kvcols = pl.ds(pl.multiple_of((h // 8) * 128, 128), 128)
        q = qbuf[:, :, cols].reshape(256, 128)
        key = kvbuf[js, :, 0, :, kvcols].reshape(512, 128)
        value = kvbuf[js, :, 1, :, kvcols].reshape(512, 128)
        s = lax.dot_general(q, key, (((1,), (1,)), ((), ())), preferred_element_type=F32)
        if masked:
            row = lax.broadcasted_iota(jnp.int32, s.shape, 0) + 256 * (j % 2)
            col = lax.broadcasted_iota(jnp.int32, s.shape, 1)
            s = jnp.where(col <= row, s, -1e30)
        old = mx[h]
        new = jnp.maximum(old, jnp.max(s, axis=1, keepdims=True))
        mx[h] = new
        scale = jnp.exp2((old - new) * factor)
        wide = jnp.concatenate([new] * 4, axis=1)
        p = jnp.exp2((s - wide) * factor).astype(BF16)
        aug = jnp.concatenate([value, jnp.ones_like(value)], axis=1)
        o = jnp.dot(p, aug, preferred_element_type=F32)
        acc[h] = acc[h] * jnp.concatenate([scale, scale], axis=1) + o

    def kv_arrived(js):
        return remote(kvbuf.at[js], kvbuf.at[js], kv_ssem.at[0], kv_rsem.at[js], partner)

    def relay(js, index, target):
        return remote(kvbuf.at[js], kvbuf.at[js], kv_ssem.at[index], kv_rsem.at[js], dev(*target, k))

    chip_z = x * 2 + 1 - z
    chip_dn = down * 2 + z
    chip_up_z = up * 2 + 1 - z
    relays = [
        relay(chip_z, 14, (up, z)),
        relay(chip_z, 15, (down, z)),
        relay(chip_dn, 16, (up, z)),
        relay(chip_up_z, 17, (down, z)),
    ]

    def step(i, carry):
        dx = jnp.where(i < 2, 0, jnp.where(i >= 6, 2, jnp.where((i == 3) | (i == 4), 1, 3)))
        dz = jnp.where((i == 1) | (i == 4) | (i == 5) | (i == 7), 1, 0)
        js = ((x + dx) % 4) * 2 + (z + dz) % 2
        kv_arrived(js).wait_recv()

        @pl.when(i == 1)
        def _():
            relays[0].start()
            relays[1].start()

        @pl.when(i == 2)
        def _():
            relays[2].start()

        @pl.when(i == 4)
        def _():
            relays[3].start()

        @pl.when(i == 5)
        def _():
            @pl.when(mine)
            def _():
                w_arrived(slot_own_z).wait_recv()
                for copy in z_sends:
                    copy.start()

            @pl.when(down_in)
            def _():
                w_arrived(slot_dn).wait_recv()
                dn_send.start()

        @pl.when(js - 4 < j // 2)
        def _():
            lax.fori_loop(0, 16, lambda h, cc: (head(h, js, False), cc)[1], 0)

        @pl.when(js - 4 == j // 2)
        def _():
            lax.fori_loop(0, 16, lambda h, cc: (head(h, js, True), cc)[1], 0)

        return carry

    lax.fori_loop(0, 8, step, 0)

    @pl.when(up_in)
    def _():
        w_arrived(slot_up_z).wait_recv()
        up_send.start()

    def finish(h, carry):
        value = acc[h]
        attn[:, pl.ds(pl.multiple_of(h * 128, 128), 128)] = (value[:, :128] / value[:, 128:]).astype(BF16)
        return carry

    lax.fori_loop(0, 16, finish, 0)

    for copy in sends[len(sends) - 3:]:
        copy.wait_recv()
    for copy in locals_[1:]:
        copy.wait()
    t_from = lax.broadcasted_iota(jnp.int32, (TOK, TOK), 0)
    t_to = lax.broadcasted_iota(jnp.int32, (TOK, TOK), 1)
    before = (t_from < t_to).astype(BF16)
    expert = 2 * lax.broadcasted_iota(jnp.int32, (CHIPS, TOK), 0) + k
    for b in range(2):
        named = jnp.zeros((CHIPS, TOK), F32)
        gate = jnp.zeros((CHIPS, TOK), F32)
        for kk in range(TOPK):
            hit = idsbuf[b, kk:kk + 1, :] == expert
            named = named + jnp.where(hit, 1.0, 0.0)
            gate = gate + jnp.where(hit, gatbuf[b, kk:kk + 1, :], 0.0)
        rank = jnp.dot(named.astype(BF16), before, preferred_element_type=F32)
        valb[:, b * TOK:(b + 1) * TOK] = named * (rank + 1.0)
        gb[:, b * TOK:(b + 1) * TOK] = gate
    u = lax.broadcasted_iota(jnp.int32, (PAIR, 256), 0)
    lane = lax.broadcasted_iota(jnp.int32, (PAIR, 256), 1)
    wanted = jnp.where(u // CAP == lane // TOK, u % CAP + 1, -1).astype(F32)

    def slot_rows(values):
        def one(ch, carry):
            rows = pl.ds(pl.multiple_of(ch * PAIR, 8), PAIR)
            match = valb[pl.ds(ch, 1), :] == wanted
            filled = gb[pl.ds(ch, 1), :] if values else 1.0
            tmp[rows, :] = jnp.where(match, filled, 0.0)
            return carry

        lax.fori_loop(0, CHIPS, one, 0)

    slot_rows(False)

    def cast(i, carry):
        rows = pl.ds(pl.multiple_of(i * 192, 192), 192)
        p_ref[rows, :] = tmp[rows, :].astype(BF16)
        return carry

    lax.fori_loop(0, 8, cast, 0)
    slot_rows(True)
    for i in range(SLOTS // 256):
        turned = tmp[i * 256:(i + 1) * 256, :].T
        top = turned.astype(BF16)
        chi_ref[:, i * 256:(i + 1) * 256] = top
        clo_ref[:, i * 256:(i + 1) * 256] = (turned - top.astype(F32)).astype(BF16)

    part[...] = jnp.zeros_like(part)
    near_par = jnp.where(mine, y % 2, 1 - y % 2)

    def slot_at(i):
        return jnp.where(i < 2, near_par, 1 - near_par) * 2 + jnp.where(i % 2 == 0, hi, 1 - hi)

    own_slot = jnp.where(mine, slot_own, -1)

    def project(i, carry):
        slot = slot_at(i)
        done_z = jnp.logical_and(mine, slot == slot_own_z)
        done_dn = jnp.logical_and(down_in, slot == slot_dn)
        done_up = jnp.logical_and(up_in, slot == slot_up_z)
        seen = jnp.logical_or(done_z, jnp.logical_or(done_dn, done_up))

        @pl.when(jnp.logical_not(seen))
        def _():
            w_arrived(slot).wait_recv()

        rows = attn[:, pl.ds(pl.multiple_of(slot * 512, 512), 512)]
        for nn in range(4):
            cols = slice(nn * 512, (nn + 1) * 512)
            part[:, cols] += jnp.dot(rows, wbuf[slot, :, cols], preferred_element_type=F32)
        return carry

    lax.fori_loop(0, 4, project, 0)
    halves = []
    for nn in range(4):
        sendb[nn] = part[:, nn * 512:(nn + 1) * 512].astype(BF16)
        copy = remote(sendb.at[nn], recvb.at[nn], pr_ssem.at[nn], pr_rsem.at[nn], partner)
        copy.start()
        halves.append(copy)
    for copy in halves:
        copy.wait_recv()

    gain = gain_ref[...]

    def normalise(i, carry):
        rows = pl.ds(pl.multiple_of(i * 32, 32), 32)
        toks = tokbuf[i // 4, pl.ds(pl.multiple_of((i % 4) * 32, 32), 32), :].astype(F32)
        other = jnp.concatenate([recvb[nn, rows, :] for nn in range(4)], axis=1).astype(F32)
        residual = (toks + part[rows, :] + other).astype(BF16)
        wide = residual.astype(F32)
        mean = jnp.mean(wide * wide, axis=1, keepdims=True)
        resid_ref[rows, :] = residual
        normed_ref[rows, :] = (wide * lax.rsqrt(mean + 1e-06) * gain).astype(BF16)
        return carry

    lax.fori_loop(0, 8, normalise, 0)

    for copy in sends:
        copy.wait_send()
    for copy in relays:
        copy.wait_send()
    for copy in halves:
        copy.wait_send()

    @pl.when(mine)
    def _():
        for copy in own_sends + z_sends:
            copy.wait_send()

    @pl.when(down_in)
    def _():
        dn_send.wait_send()

    @pl.when(up_in)
    def _():
        up_send.wait_send()


def attention(tokens, queries, keys_values, out_weight, moe_gain, expert_ids, gates):
    dma = pltpu.SemaphoreType.DMA
    anywhere = pl.BlockSpec(memory_space=pl.ANY)
    vmem = pl.BlockSpec(memory_space=pltpu.VMEM)
    return pl.pallas_call(
        attn_kernel,
        name="attend",
        out_shape=(
            jax.ShapeDtypeStruct((256, D), BF16),
            jax.ShapeDtypeStruct((256, D), BF16),
            jax.ShapeDtypeStruct((SLOTS, 256), BF16),
            jax.ShapeDtypeStruct((256, SLOTS), BF16),
            jax.ShapeDtypeStruct((256, SLOTS), BF16),
        ),
        in_specs=[anywhere] * 4 + [vmem] * 3,
        out_specs=(vmem,) * 5,
        scratch_shapes=[
            pltpu.VMEM((8, 2, 2, 256, 256), BF16),
            pltpu.VMEM((2, TOK, 2048), BF16),
            pltpu.VMEM((2, TOK, D), BF16),
            pltpu.VMEM((2, TOPK, TOK), jnp.int32),
            pltpu.VMEM((2, TOPK, TOK), F32),
            pltpu.VMEM((4, 512, D), BF16),
            pltpu.VMEM((16, 256, 256), F32),
            pltpu.VMEM((16, 256, 128), F32),
            pltpu.VMEM((256, 2048), BF16),
            pltpu.VMEM((256, D), F32),
            pltpu.VMEM((4, 256, 512), BF16),
            pltpu.VMEM((4, 256, 512), BF16),
            pltpu.VMEM((SLOTS, 256), F32),
            pltpu.VMEM((CHIPS, 256), F32),
            pltpu.VMEM((CHIPS, 256), F32),
            dma((18,)), dma((8,)), dma((7,)), dma((4,)), dma((8,)), dma((4,)), dma((4,)), dma((4,)),
        ],
        compiler_params=pltpu.CompilerParams(
            collective_id=0, has_side_effects=True, vmem_limit_bytes=60 * 1024 * 1024
        ),
    )(tokens, queries, keys_values, out_weight, moe_gain.reshape(1, D), expert_ids.T, gates.T)


def per_device(
    tokens,
    queries,
    keys_values,
    out_weight,
    moe_gain,
    expert_ids,
    gates,
    w_gate_experts,
    w_up_experts,
    w_down_experts,
):
    tok_count = tokens.shape[0]
    resid2, normed2, _, _, _ = attention(
        tokens, queries, keys_values, out_weight, moe_gain, expert_ids, gates
    )
    start = (lax.axis_index("ctx") % 2) * TOK
    residual = lax.dynamic_slice_in_dim(resid2, start, TOK, 0)
    normed = lax.dynamic_slice_in_dim(normed2, start, TOK, 0)
    wide = residual.astype(jnp.float32)
    flat_ids = expert_ids.reshape(-1)
    one_hot = (flat_ids[:, None] == jnp.arange(EXPERTS, dtype=jnp.int32)[None, :]).astype(jnp.int32)
    slot_index = jnp.sum((jnp.cumsum(one_hot, axis=0) - one_hot) * one_hot, axis=1)
    position = flat_ids * CAP + slot_index
    token_index = jnp.arange(tok_count * TOPK, dtype=jnp.int32) // TOPK
    table = jnp.full((EXPERTS * CAP,), tok_count, jnp.int32).at[position].set(token_index)
    present = table < tok_count
    outgoing = jnp.where(present[:, None], normed[jnp.minimum(table, tok_count - 1)], 0.0)
    local_experts = w_gate_experts.shape[0]
    owners = EXPERTS // local_experts
    width = normed.shape[1]
    outgoing = outgoing.reshape(owners, local_experts, CAP, width)
    incoming = lax.all_to_all(outgoing, ("grp", "ctx"), split_axis=0, concat_axis=0, tiled=True)
    gate_part = jnp.einsum(
        "sjcd,jdf->sjcf", incoming, w_gate_experts, preferred_element_type=jnp.float32
    )
    up_part = jnp.einsum(
        "sjcd,jdf->sjcf", incoming, w_up_experts, preferred_element_type=jnp.float32
    )
    hidden = (jax.nn.silu(gate_part) * up_part).astype(jnp.bfloat16)
    result_rows = jnp.einsum(
        "sjcf,jfd->sjcd", hidden, w_down_experts, preferred_element_type=jnp.float32
    ).astype(jnp.bfloat16)
    returned = lax.all_to_all(result_rows, ("grp", "ctx"), split_axis=0, concat_axis=0, tiled=True)
    picked = returned.reshape(EXPERTS * CAP, width)[position].reshape(tok_count, TOPK, width)
    combined = jnp.sum(picked.astype(jnp.float32) * gates[:, :, None], axis=1)
    return (wide + combined).astype(jnp.bfloat16)


def solution(mesh):
    return jax.shard_map(
        per_device,
        mesh=mesh,
        in_specs=(
            P(("grp", "ctx"), None),
            P(("grp", "ctx"), None),
            P("grp", "ctx", None),
            P("grp", None),
            P(),
            P(("grp", "ctx"), None),
            P(("grp", "ctx"), None),
            P(("grp", "ctx"), None, None),
            P(("grp", "ctx"), None, None),
            P(("grp", "ctx"), None, None),
        ),
        out_specs=P(("grp", "ctx"), None),
        check_vma=False,
    )
```

time: 694 us -> 462 us (0.67)
  waiting for transfers between devices: 246 us -> 112 us
  Pallas kernels: 0 us -> 103 us
  matrix products: 123 us -> 30.5 us
  other arithmetic: 59.1 us -> 18.2 us
  local copies, waits for them, and re-layouts: 102 us -> 64.1 us
  blocking collectives: 133 us -> 119 us
  between operations: 14.2 us -> 0.77 us
    pallas_call x0 -> x1, Pallas kernels: none -> 103 us  [attention(): pl.pallas_call(attn_kernel, name='attend', out_shape=(jax.ShapeDtypeStruc...]
    dot_general x9 -> x0, matrix products: 92.8 us -> none  [the longest x4 43.9 us: softmax_step(): jnp.einsum('gqk,gkd->gqd', weights, value_block, preferred_element_type=j...]
    reduce_scatter x1 -> x0, waiting for transfers between devices: 73.5 us -> none  [per_device(): lax.psum_scatter(jnp.dot(head_parts, out_weight, preferred_element_type=j...]
    all_gather x1 -> x0, waiting for transfers between devices: 60.1 us -> none  [per_device(): piece = lax.all_gather(keys_values, 'ctx', axis=1, tiled=True)]
    reduce_sum x5 -> x0, other arithmetic: 33.8 us -> none  [the longest x4 32.4 us: softmax_step(): jnp.sum(weights, axis=2, dtype=jnp.float32)]
    all_to_all x1 -> x0, blocking collectives: 23.9 us -> none  [per_device(): lax.all_to_all(attended, 'grp', split_axis=1, concat_axis=0, tiled=True)]
    reshape x9 -> x0, local copies, waits for them, and re-layouts: 19.5 us -> none  [the longest x4 9.08 us: one_block(): window[:, kv_width:].reshape(block_size, KV_HEADS, HEAD_DIM)]
    all_to_all x1, blocking collectives: 109 us -> 119 us  [per_device(): lax.all_to_all(outgoing, ('grp', 'ctx'), split_axis=0, concat_axis=0, til...]
  transfers between devices with their start and end apart: 3 -> 1, of which waited for: 3 -> 1; matrix products, arithmetic and copies ran while one was open for 2% -> 0% of each run, Pallas kernels for 0% -> 0%
where the time goes in v1:
time: 462 us; the launch traced here: 454 us
  blocking collectives  119 us (26%)
  waiting for transfers between devices  112 us (24%)
  Pallas kernels  103 us (22%)
  local copies, waits for them, and re-layouts  64.1 us (14%)
  matrix products  30.5 us (7%)
  other arithmetic  18.2 us (4%)
  starting transfers between devices  6.97 us (2%)
    all_to_all x1, blocking collectives, per_device(): lax.all_to_all(outgoing, ('grp', 'ctx'), split_axis=0, concat_axis=0, til...  119 us
    all_to_all x1, waiting for transfers between devices, per_device(): lax.all_to_all(result_rows, ('grp', 'ctx'), split_axis=0, concat_axis=0,...  112 us
    pallas_call x1, Pallas kernels, attention(): pl.pallas_call(attn_kernel, name='attend', out_shape=(jax.ShapeDtypeStruc...  103 us
    gather x2, local copies, waits for them, and re-layouts, per_device(): normed[jnp.minimum(table, tok_count - 1)]  24.4 us
    dot_general x1, matrix products, per_device(): jnp.einsum('sjcd,jdf->sjcf', incoming, w_up_experts, preferred_element_ty...  12.7 us
    gather x1, local copies, waits for them, and re-layouts, per_device(): returned.reshape(EXPERTS * CAP, width)[position]  12.6 us
    dot_general x1, matrix products, per_device(): jnp.einsum('sjcd,jdf->sjcf', incoming, w_gate_experts, preferred_element_...  12.5 us
    reshape x1, local copies, waits for them, and re-layouts, per_device(): returned.reshape(EXPERTS * CAP, width)[position]  10.7 us
  transfers between devices with their start and end apart: 1, of which 1 were waited for; matrix products, arithmetic and copies ran while one was open for 0% of the time, Pallas kernels for 0%

profile of v1, /device:TPU:4, one launch (start us, length us, event | category | flops | bytes accessed | tf_op | source)
XLA Modules:
  0.0 454.5 jit_solution(18008398862629946174)
XLA Ops:
  0.0 0.9 copy.22
  1.1 0.7 broadcast_multiply_fusion
  1.9 0.2 fusion.18
  2.1 0.8 copy-done.2
  3.0 1.1 broadcast_add_fusion
  4.0 0.9 copy.25
  5.1 1.4 fusion.17
  6.5 4.3 scatter_custom_fusion
  10.9 102.9 %attend.1 = (bf16[256,2048]{1,0:T(8,128)(2,1)}, bf16[256,2048]{1,0:T(8,128)(2,1)}, bf16[1536,256]{1,0:T(8,128)(2,1)}, bf16[256,1536]{1,0:T(8,128)(2,1)}, bf16[256,1536]{1,0:T(8,128)(2,1)}) custom-call(bf16[128,2048]{1,0:T(8,128)(2,1)} %tok_hbm.1, bf16[128,4096]{1,0:T(8,128)(2,1)} %q_hbm.1, bf16[1,256,1024]{2,1,0:T(8,128)(2,1)} %kv_hbm.1, ...), custom_call_target="tpu_custom_call" | custom-call | tf_op jit(solution)/shard_map/attend/pallas_call | solution.py:358
  113.9 1.9 constant_dynamic-slice_fusion
  115.7 13.8 %gather_fusion = bf16[1536,2048]{1,0:T(8,128)(2,1)} fusion(bf16[128,2048]{1,0:T(8,128)(2,1)} %constant_dynamic-slice_fusion, s32[2048]{0:T(1024)S(1)} %pad_clamp_fusion), kind=kCustom, calls=%fused_computation | custom fusion | bytes 12589056 | tf_op jit(solution)/shard_map/gather | solution.py:421
  129.5 10.6 %gather.9 = bf16[128,1,12,2048]{3,2,0,1:T(8,128)(2,1)} reshape(bf16[1536,2048]{1,0:T(8,128)(2,1)} %gather_fusion) | data formatting | bytes 12582912 | tf_op jit(solution)/shard_map/gather | solution.py:421
  140.3 7.3 %select_bitcast_fusion = bf16[128,1,12,2048]{3,2,1,0:T(8,128)(2,1)} fusion(bf16[128,1,12,2048]{3,2,0,1:T(8,128)(2,1)} %gather.9, pred[128,12]{1,0:T(8,128)(4,1)S(1)} %broadcast_in_dim.22), kind=kLoop, calls=%fused_computation.5 | loop fusion | flops 3145728 | bytes 12584448 | tf_op jit(solution)/shard_map/jit(_where)/select_n | solution.py:421
  147.5 119.1 %all_to_all.10 = bf16[128,1,12,2048]{3,2,1,0:T(8,128)(2,1)S(1)} all-to-all(bf16[128,1,12,2048]{3,2,1,0:T(8,128)(2,1)} %select_bitcast_fusion), channel_id=1, replica_groups=mesh['grp'=8,'ctx'=16] {'grp','ctx'}, dimensions={0} | all-to-all | bytes 12582912 | tf_op jit(solution)/shard_map/all_to_all | solution.py:426
  266.7 12.7 %fusion.1 = f32[128,12,768]{2,0,1:T(8,128)S(1)} fusion(bf16[128,1,12,2048]{3,2,1,0:T(8,128)(2,1)S(1)} %all_to_all.10, bf16[1,2048,768]{2,1,0:T(8,128)(2,1)S(1)} %copy-done.5), kind=kOutput, calls=%fused_computation.6 | convolution fusion | flops 4831838208 | bytes 14155776 | tf_op jit(solution)/shard_map/sjcd,jdf->sjcf/dot_general | solution.py:430
  279.4 12.5 %fusion.3 = f32[128,12,768]{2,0,1:T(8,128)S(1)} fusion(bf16[128,1,12,2048]{3,2,1,0:T(8,128)(2,1)S(1)} %all_to_all.10, bf16[1,2048,768]{2,1,0:T(8,128)(2,1)S(1)} %copy-done.6), kind=kOutput, calls=%fused_computation.8 | convolution fusion | flops 4831838208 | bytes 14155776 | tf_op jit(solution)/shard_map/sjcd,jdf->sjcf/dot_general | solution.py:427
  292.2 5.3 %convert_bitcast_fusion = bf16[128,1,12,2048]{3,0,2,1:T(8,128)(2,1)S(1)} fusion(bf16[1,768,2048]{2,1,0:T(8,128)(2,1)S(1)} %copy-done, f32[128,12,768]{2,0,1:T(8,128)S(1)} %fusion.1, f32[128,12,768]{2,0,1:T(8,128)S(1)} %fusion.3), kind=kOutput, calls=%fused_computation.10 | convolution fusion | flops 4842061824 | bytes 18874368 | tf_op jit(solution)/shard_map/sjcf,jfd->sjcd/dot_general | solution.py:434
  297.6 6.8 %copy.28 = bf16[128,1,12,2048]{3,2,1,0:T(8,128)(2,1)} copy(bf16[128,1,12,2048]{3,0,2,1:T(8,128)(2,1)S(1)} %convert_bitcast_fusion) | data formatting | bytes 12582912 | tf_op jit(solution)/shard_map/convert_element_type | solution.py:436
  304.4 7.0 %all-to-all-start.1 = ((bf16[128,1,12,2048]{3,2,1,0:T(8,128)(2,1)}), bf16[128,1,12,2048]{3,2,1,0:T(8,128)(2,1)}, u32[]{:S(2)}, u32[]{:S(2)}) async-start(bf16[128,1,12,2048]{3,2,1,0:T(8,128)(2,1)} %copy.28), calls=%async_computation.1 | async-start | bytes 16777216 | tf_op jit(solution)/shard_map/all_to_all | solution.py:437
  311.5 111.9 %all-to-all-done.1 = bf16[128,1,12,2048]{3,2,1,0:T(8,128)(2,1)} async-done(((bf16[128,1,12,2048]{3,2,1,0:T(8,128)(2,1)}), bf16[128,1,12,2048]{3,2,1,0:T(8,128)(2,1)}, u32[]{:S(2)}, u32[]{:S(2)}) %all-to-all-start.1) | async-done | bytes 6291488 | tf_op jit(solution)/shard_map/all_to_all | solution.py:437
  423.5 10.7 %reshape.102 = bf16[1536,2048]{1,0:T(8,128)(2,1)} reshape(bf16[128,1,12,2048]{3,2,1,0:T(8,128)(2,1)} %all-to-all-done.1) | data formatting | bytes 12582912 | tf_op jit(solution)/shard_map/reshape | solution.py:438
  434.2 12.6 %gather_fusion.1 = bf16[1024,2048]{1,0:T(8,128)(2,1)} fusion(bf16[1536,2048]{1,0:T(8,128)(2,1)} %reshape.102, s32[1024]{0:T(1024)S(1)} %broadcast_clamp_fusion), kind=kCustom, calls=%fused_computation.1 | custom fusion | bytes 8392704 | tf_op jit(solution)/shard_map/gather | solution.py:438
  446.7 6.6 %fusion = f32[128,2048]{1,0:T(8,128)S(1)} fusion(bf16[1024,2048]{1,0:T(8,128)(2,1)} %gather_fusion.1, f32[128,8]{1,0:T(8,128)S(1)} %copy.29), kind=kLoop, calls=%fused_computation.4 | loop fusion | flops 6029312 | bytes 5246976 | tf_op jit(solution)/shard_map/reduce_sum | solution.py:439
  453.4 0.9 add_convert_fusion
  (29 shorter events, 0.8 us)
Async XLA Ops:
  0.0 292.2 %copy-start = (bf16[1,768,2048]{2,1,0:T(8,128)(2,1)S(1)}, bf16[1,768,2048]{2,1,0:T(8,128)(2,1)}, u32[]{:S(2)}) copy-start(bf16[1,768,2048]{2,1,0:T(8,128)(2,1)} %param.19) | copy-start | bytes 9437188
  2.1 0.8 copy-start.2
  147.5 119.1 %copy-start.5 = (bf16[1,2048,768]{2,1,0:T(8,128)(2,1)S(1)}, bf16[1,2048,768]{2,1,0:T(8,128)(2,1)}, u32[]{:S(2)}) copy-start(bf16[1,2048,768]{2,1,0:T(8,128)(2,1)} %param.18) | copy-start | bytes 9437188
  266.7 12.7 %copy-start.6 = (bf16[1,2048,768]{2,1,0:T(8,128)(2,1)S(1)}, bf16[1,2048,768]{2,1,0:T(8,128)(2,1)}, u32[]{:S(2)}) copy-start(bf16[1,2048,768]{2,1,0:T(8,128)(2,1)} %param.17) | copy-start | bytes 9437188
  304.4 7.0 %copy-start.4 = (f32[128,8]{0,1:T(8,128)S(1)}, f32[128,8]{0,1:T(8,128)}, u32[]{:S(2)}) copy-start(f32[128,8]{0,1:T(8,128)} %param.16) | copy-start | bytes 12292
  304.4 119.0 %all-to-all-start.1 = ((bf16[128,1,12,2048]{3,2,1,0:T(8,128)(2,1)}), bf16[128,1,12,2048]{3,2,1,0:T(8,128)(2,1)}, u32[]{:S(2)}, u32[]{:S(2)}) async-start(bf16[128,1,12,2048]{3,2,1,0:T(8,128)(2,1)} %copy.28), calls=%async_computation.1 | async-start | bytes 16777216 | tf_op jit(solution)/shard_map/all_to_all | solution.py:437
  434.2 20.1 %copy-start.1 = (bf16[1,768,2048]{2,1,0:T(8,128)(2,1)S(1)}, bf16[1,768,2048]{2,1,0:T(8,128)(2,1)}, u32[]{:S(2)}) copy-start(bf16[1,768,2048]{2,1,0:T(8,128)(2,1)} %param.19) | copy-start | bytes 9437188
  446.7 6.6 %copy-start.3 = (bf16[256,2048]{1,0:T(8,128)(2,1)S(1)}, bf16[256,2048]{1,0:T(8,128)(2,1)}, u32[]{:S(2)}) copy-start(bf16[256,2048]{1,0:T(8,128)(2,1)} %get-tuple-element.7) | copy-start | bytes 3145732
